TPU v7x, 128 devices: a whole 4x4x4 slice. The times are simulated.
128 devices in a mesh: row: 64 (over z, y, x), col: 2 (over core).
Axes of the slice: x: 4, y: 4, z: 4, core: 2. Of those that a mesh axis runs over, the one named last changes fastest.
Arguments:
- vectors_in: bfloat16 [131072, 2048], P('row', 'col'), may hold values from -6 to 6
- panel: bfloat16 [131072, 256], P('row', 'col'), may hold values from -0.015625 to 0.015625
- factor: float32 [256, 256], replicated, may hold values from -3 to 8, as said below
- atom_basis: int32 [64, 128], P('row'), may hold values from 1 to 24, 2048 in all within a row
- proj_count: int32 [8192], P('row'), may hold values from 1 to 16
- coupling: bfloat16 [8192, 9, 384], P('row'), may hold values from -0.4375 to 0.4375
- block_present: int32 [8192, 9], P('row'), may hold values 0 or 1
- occ_mask: int32 [2048], P('col'), may hold values 0 or 1
- occ_weight: float32 [2048], P('col'), may hold values from 0.5 to 2
Outputs:
- vectors: bfloat16 [131072, 2048], P('row', 'col')
- density: float32 [8192, 256], P(('row', 'col'))
Inputs may be any that keep to these rules, and one draw needn't show every extreme that they name: `factor`: zero below the diagonal; the diagonal lies in 4 to 8. `atom_basis`: each row sums to 2048, and 24 is reached in each row.
All inputs are finite; a program needn't handle non-finite values. No bound on the sum of `block_present` or of `occ_mask` on one device may be relied on, other than what follows from the above.
Results may differ from a plain program's by a relative error of at most 0.0075.
Values may be sent and summed in bfloat16 or wider, within the bound.
No kernel may reach another device: no remote copies, remote signals or barrier semaphores. Data moves between devices by JAX's collectives and lax.ppermute only.
A program may use at most 192 MiB of HBM per device.

v0:
```python
import jax
import jax.numpy as jnp
from jax import lax
from jax.sharding import PartitionSpec as P

NPMAX = 16
BMAX = 24
K = 9


def with_halo(array, sides, width):
    for axis, dim in sides:
        devices, length = (lax.axis_size(axis), array.shape[dim])
        up = [(i, (i + 1) % devices) for i in range(devices)]
        down = [(j, i) for i, j in up]
        last = lax.slice_in_dim(array, length - width, length, axis=dim)
        first = lax.slice_in_dim(array, 0, width, axis=dim)
        before = lax.ppermute(last, axis, up)
        after = lax.ppermute(first, axis, down)
        array = jnp.concatenate([before, array, after], axis=dim)
    return array


def panel_product(fragment, columns):
    return lax.dot_general(
        fragment, columns, (((0,), (0,)), ((), ())), preferred_element_type=jnp.float32
    )


def local(
    vectors_in, panel, factor, atom_basis, proj_count, coupling, block_present, occ_mask, occ_weight
):
    rows_here = vectors_in.shape[0]
    cols_here = vectors_in.shape[1]
    whole_panel = lax.all_gather(panel, "col", axis=1, tiled=True)
    inner_products = panel_product(whole_panel, vectors_in)
    inner_products = lax.psum(inner_products, "row")
    mixing = jnp.dot(factor.T, inner_products, precision=lax.Precision.HIGHEST).astype(jnp.bfloat16)
    update = jnp.dot(whole_panel, mixing, preferred_element_type=jnp.float32)
    vectors = (vectors_in.astype(jnp.float32) - update).astype(jnp.bfloat16)
    counts = atom_basis[0]
    atoms_here = counts.shape[0]
    starts = jnp.cumsum(counts) - counts
    slot_rank = jnp.arange(BMAX, dtype=jnp.int32)
    row_index = jnp.where(
        slot_rank[None, :] < counts[:, None], starts[:, None] + slot_rank[None, :], rows_here
    )
    padded = jnp.take(vectors, row_index.reshape(-1), axis=0, mode="fill", fill_value=0).reshape(
        atoms_here, BMAX, cols_here
    )
    rim_width = (K - 1) // 2
    extended = with_halo(padded, (("row", 0),), rim_width)
    projections = jnp.zeros((atoms_here, NPMAX, cols_here), jnp.float32)
    for relative in range(K):
        blocks = coupling[:, relative].reshape(atoms_here, NPMAX, BMAX)
        blocks = jnp.where(
            block_present[:, relative, None, None] > 0, blocks, jnp.zeros_like(blocks)
        )
        neighbours = extended[relative : relative + atoms_here]
        projections = projections + jnp.einsum(
            "aij,ajn->ain", blocks, neighbours, preferred_element_type=jnp.float32
        )
    kept_rows = (jnp.arange(NPMAX, dtype=jnp.int32)[None, :] < proj_count[:, None]).astype(
        jnp.float32
    )
    rounded = (projections * kept_rows[:, :, None]).astype(jnp.bfloat16)
    column_total = cols_here * lax.axis_size("col")
    weights = occ_mask.astype(jnp.float32) * occ_weight / column_total
    weighted = (rounded * weights[None, None, :]).astype(jnp.bfloat16)
    partial_value = jnp.einsum(
        "ain,ajn->aij", weighted, rounded, preferred_element_type=jnp.float32
    )
    partial_value = partial_value.reshape(atoms_here, NPMAX * NPMAX)
    summed = lax.psum(partial_value.astype(jnp.bfloat16), "col").astype(jnp.float32)
    per_device = atoms_here // lax.axis_size("col")
    density = lax.dynamic_slice_in_dim(summed, lax.axis_index("col") * per_device, per_device, 0)
    return (vectors, density)


def solution(mesh):
    placed = (
        P("row", "col"),
        P("row", "col"),
        P(),
        P("row", None),
        P("row"),
        P("row", None, None),
        P("row", None),
        P("col"),
        P("col"),
    )
    return jax.shard_map(
        local,
        mesh=mesh,
        in_specs=placed,
        out_specs=(P("row", "col"), P(("row", "col"), None)),
        check_vma=False,
    )
```

profile of v0, /device:TPU:1, one launch (start us, length us, event | category | flops | bytes accessed | tf_op | source)
XLA Modules:
  0.0 322.8 jit_solution(1924844101190805468)
XLA Ops:
  7.2 0.0 copy-start
  7.2 0.0 all-gather.2.cloned.1.call-start
  7.2 0.7 all-gather.2.cloned.1.call-update
  7.9 0.0 all-reduce.3.cloned.1.call-start
  8.0 0.8 copy.17
  8.7 0.2 reduce-window.8
  8.9 0.1 reduce
  9.0 0.7 bitcast_subtract_fusion.1
  9.7 0.8 add_select_fusion
  10.4 0.1 select_n.82
  10.5 0.1 select_n.80
  10.6 1.4 fusion.48
  12.0 0.1 copy.41
  12.1 0.1 copy.42
  12.2 1.0 compare_bitcast_fusion.7
  13.3 0.4 copy.23
  13.7 0.0 copy-start.12
  13.7 0.0 copy-start.10
  13.7 6.4 %copy.15 = bf16[2048,1024]{0,1:T(8,128)(2,1)} copy(bf16[2048,1024]{1,0:T(8,128)(2,1)} %param.9) | data formatting | bytes 8388608 | tf_op args[0]
  20.2 0.1 copy.39
  20.3 0.1 copy.40
  20.5 1.2 copy.19
  21.7 1.2 copy.21
  22.9 0.4 copy.25
  23.3 0.1 copy.44
  23.4 0.1 copy.45
  23.6 1.2 copy.29
  24.8 1.2 copy.31
  26.0 0.1 copy.46
  26.1 0.1 copy.47
  26.3 1.2 copy.33
  27.4 0.4 copy.35
  27.9 0.1 copy.43
  28.0 0.4 copy.27
  28.5 0.1 compare_and_fusion
  28.6 0.0 all-gather.2.cloned.1.call-done
  28.7 4.9 %fusion.51 = f32[256,1024]{1,0:T(8,128)} fusion(bf16[2048,256]{1,0:T(8,128)(2,1)} %all-gather.2.cloned.1.call-done, bf16[2048,1024]{1,0:T(8,128)(2,1)} %param.9), kind=kOutput, calls=%fused_computation.89 | convolution fusion | flops 1073741824 | bytes 6291456 | tf_op jit(solution)/shard_map/dot_general | solution.py:25
  33.5 0.0 all-reduce.3.cloned.1.call-update
  33.6 0.0 all-reduce.5.cloned.1.call-start
  33.7 0.1 fusion.38
  33.7 130.9 %all-reduce.3.cloned.1.call-done = f32[256,1024]{1,0:T(8,128)} async-done(((f32[256,1024]{1,0:T(8,128)}), f32[256,1024]{1,0:T(8,128)}) %all-reduce.3.cloned.1.call-update) | async-done | bytes 1048592 | tf_op jit(solution)/shard_map/psum | solution.py:37
  164.7 3.0 convolution_convert_fusion
  167.7 5.4 %fusion = bf16[2048,1024]{0,1:T(8,128)(2,1)} fusion(bf16[2048,1024]{0,1:T(8,128)(2,1)} %copy.15, bf16[1024,256]{1,0:T(8,128)(2,1)S(1)} %convolution_convert_fusion, bf16[2048,256]{1,0:T(8,128)(2,1)S(1)} %copy-done.4), kind=kOutput, calls=%fused_computation.8 | convolution fusion | flops 1080033280 | bytes 9961472 | tf_op jit(solution)/shard_map/dot_general | solution.py:39
  173.2 6.4 %copy.37 = bf16[2048,1024]{1,0:T(8,128)(2,1)} copy(bf16[2048,1024]{0,1:T(8,128)(2,1)} %fusion) | data formatting | bytes 8388608
  179.5 18.7 %gather_fusion = bf16[3072,1024]{1,0:T(8,128)(2,1)} fusion(bf16[2048,1024]{1,0:T(8,128)(2,1)} %copy.37, s32[3072]{0:T(1024)S(1)} %broadcast_clamp_fusion), kind=kCustom, calls=%fused_computation | custom fusion | bytes 12595200 | tf_op jit(solution)/shard_map/jit(_take)/gather | solution.py:48
  198.2 4.1 %broadcast_select_fusion = bf16[3072,1024]{1,0:T(8,128)(2,1)S(1)} fusion(bf16[3072,1024]{1,0:T(8,128)(2,1)} %gather_fusion, pred[3072]{0:T(1024)(128)(4,1)S(1)} %compare_and_fusion.1), kind=kLoop, calls=%fused_computation.36 | loop fusion | flops 3145728 | bytes 12585984 | tf_op jit(solution)/shard_map/jit(_take)/select_n | solution.py:48
  202.3 0.8 collective-permute-start
  203.1 6.2 %collective-permute-start.1 = (bf16[4,24,1024]{2,1,0:T(8,128)(2,1)S(1)}, bf16[4,24,1024]{2,1,0:T(8,128)(2,1)S(1)}, u32[]{:S(2)}, u32[]{:S(2)}) collective-permute-start(bf16[4,24,1024]{2,1,0:T(8,128)(2,1)S(1)} %bitcast.68), channel_id=1, source_target_pairs={{2,0},{4,2},{6,4},{8,6},{10,8},{12,10},{14,12},{16,14},{18,16},{20... | collective-permute-start | bytes 589832 | tf_op jit(solution)/shard_map/ppermute | solution.py:19
  209.3 0.7 broadcast_select_fusion.1
  210.0 2.3 collective-permute-done
  212.3 4.3 %fusion.12 = f32[128,16,1024]{2,1,0:T(8,128)} fusion(bf16[128,16,24]{2,1,0:T(8,128)(2,1)S(1)} %copy.23, bf16[4,24,1024]{2,1,0:T(8,128)(2,1)S(1)} %collective-permute-done, bf16[128,24,1024]{2,1,0:T(8,128)(2,1)S(1)} %broadcast_select_fusion.1), kind=kOutput, calls=%fused_computation.19 | convolution fusion | flops 103809024 | bytes 14974976 | tf_op jit(solution)/shard_map/aij,ajn->ain/dot_general | solution.py:60
  216.6 4.3 %fusion.15 = f32[128,16,1024]{2,1,0:T(8,128)} fusion(bf16[128,16,24]{2,1,0:T(8,128)(2,1)S(1)} %copy-done.5, bf16[4,24,1024]{2,1,0:T(8,128)(2,1)S(1)} %collective-permute-done, bf16[128,24,1024]{2,1,0:T(8,128)(2,1)S(1)} %broadcast_select_fusion.1), kind=kOutput, calls=%fused_computation.21 | convolution fusion | flops 103809024 | bytes 14974976 | tf_op jit(solution)/shard_map/aij,ajn->ain/dot_general | solution.py:60
  220.9 4.3 %fusion.18 = f32[128,16,1024]{2,1,0:T(8,128)} fusion(bf16[128,16,24]{2,1,0:T(8,128)(2,1)S(1)} %copy-done.6, bf16[4,24,1024]{2,1,0:T(8,128)(2,1)S(1)} %collective-permute-done, bf16[128,24,1024]{2,1,0:T(8,128)(2,1)S(1)} %broadcast_select_fusion.1), kind=kOutput, calls=%fused_computation.23 | convolution fusion | flops 103809024 | bytes 14974976 | tf_op jit(solution)/shard_map/aij,ajn->ain/dot_general | solution.py:60
  225.2 4.3 %fusion.25 = f32[128,16,1024]{2,1,0:T(8,128)} fusion(bf16[128,16,24]{2,1,0:T(8,128)(2,1)S(1)} %copy.25, bf16[128,24,1024]{2,1,0:T(8,128)(2,1)S(1)} %broadcast_select_fusion.1, bf16[4,24,1024]{2,1,0:T(8,128)(2,1)S(1)} %collective-permute-done), kind=kOutput, calls=%fused_computation.31 | convolution fusion | flops 103809024 | bytes 14974976 | tf_op jit(solution)/shard_map/aij,ajn->ain/dot_general | solution.py:60
  229.5 4.3 %fusion.6 = f32[128,16,1024]{2,1,0:T(8,128)} fusion(bf16[128,16,24]{2,1,0:T(8,128)(2,1)S(1)} %copy-done.7, bf16[4,24,1024]{2,1,0:T(8,128)(2,1)S(1)} %collective-permute-done.1, bf16[128,24,1024]{2,1,0:T(8,128)(2,1)S(1)} %broadcast_select_fusion.1), kind=kOutput, calls=%fused_computation.15 | convolution fusion | flops 103809024 | bytes 14974976 | tf_op jit(solution)/shard_map/aij,ajn->ain/dot_general | solution.py:60
  233.8 4.3 %fusion.9 = f32[128,16,1024]{2,1,0:T(8,128)} fusion(bf16[128,16,24]{2,1,0:T(8,128)(2,1)S(1)} %copy-done.8, bf16[4,24,1024]{2,1,0:T(8,128)(2,1)S(1)} %collective-permute-done.1, bf16[128,24,1024]{2,1,0:T(8,128)(2,1)S(1)} %broadcast_select_fusion.1), kind=kOutput, calls=%fused_computation.17 | convolution fusion | flops 103809024 | bytes 14974976 | tf_op jit(solution)/shard_map/aij,ajn->ain/dot_general | solution.py:60
  238.1 4.3 %fusion.3 = f32[128,16,1024]{2,1,0:T(8,128)} fusion(bf16[128,16,24]{2,1,0:T(8,128)(2,1)S(1)} %copy-done.9, bf16[4,24,1024]{2,1,0:T(8,128)(2,1)S(1)} %collective-permute-done.1, bf16[128,24,1024]{2,1,0:T(8,128)(2,1)S(1)} %broadcast_select_fusion.1), kind=kOutput, calls=%fused_computation.13 | convolution fusion | flops 103809024 | bytes 14974976 | tf_op jit(solution)/shard_map/aij,ajn->ain/dot_general | solution.py:60
  242.4 4.3 %fusion.20 = f32[128,16,1024]{2,1,0:T(8,128)} fusion(bf16[128,16,24]{2,1,0:T(8,128)(2,1)S(1)} %copy.35, bf16[4,24,1024]{2,1,0:T(8,128)(2,1)S(1)} %collective-permute-done.1, bf16[128,24,1024]{2,1,0:T(8,128)(2,1)S(1)} %broadcast_select_fusion.1), kind=kOutput, calls=%fused_computation.25 | convolution fusion | flops 103809024 | bytes 14974976 | tf_op jit(solution)/shard_map/aij,ajn->ain/dot_general | solution.py:60
  246.7 46.4 %fusion.37 = bf16[128,16,16]{2,1,0:T(8,128)(2,1)S(1)} fusion(f32[128,16,1024]{2,1,0:T(8,128)} %fusion.20, f32[128,16,1024]{2,1,0:T(8,128)} %fusion.3, f32[128,16,1024]{2,1,0:T(8,128)} %fusion.9, f32[128,16,1024]{2,1,0:T(8,128)} %fusion.6, f32[128,16,1024]{2,1,0:T(8,128)} %fusion.25, f32[128,16,1024]{2,1,0:T(8,128)} %fusion.12, ...), kind=kOutput, calls=%fused_computation.46 | convolution fusion | flops 316702720 | bytes 73576448 | tf_op jit(solution)/shard_map/ain,ajn->aij/dot_general | solution.py:70
  293.0 1.1 copy.36
  294.1 0.0 all-reduce.5.cloned.1.call-update
  294.1 20.5 %all-reduce.5.cloned.1.call-done = bf16[128,256]{0,1:T(8,128)(2,1)} async-done(((bf16[128,256]{0,1:T(8,128)(2,1)}), bf16[128,256]{0,1:T(8,128)(2,1)}) %all-reduce.5.cloned.1.call-update) | async-done | bytes 65552 | tf_op jit(solution)/shard_map/psum | solution.py:74
  314.6 0.9 dynamic-slice_convert_fusion
  315.5 0.7 copy.38
  (36 shorter events, 0.2 us)
Async XLA Ops:
  7.2 157.5 %copy-start = (f32[256,256]{1,0:T(8,128)S(1)}, f32[256,256]{1,0:T(8,128)}, u32[]{:S(2)}) copy-start(f32[256,256]{1,0:T(8,128)} %param.11) | copy-start | bytes 786436
  7.2 21.5 %all-gather.2.cloned.1.call-start = ((), (), s32[]{:S(2)}) async-start(), calls=%async_computation | async-start | bytes 1572864 | tf_op jit(solution)/shard_map/all_gather | solution.py:35
  7.9 156.8 %all-reduce.3.cloned.1.call-start = ((), (), s32[]{:S(2)}) async-start(), calls=%async_computation.1 | async-start | bytes 2097152 | tf_op jit(solution)/shard_map/psum | solution.py:37
  13.7 14.8 %copy-start.11 = (f32[1024]{0:T(1024)S(1)}, f32[1024]{0:T(1024)}, u32[]{:S(2)}) copy-start(f32[1024]{0:T(1024)} %param.17) | copy-start | bytes 12292
  13.7 14.8 %copy-start.12 = (s32[1024]{0:T(1024)S(1)}, s32[1024]{0:T(1024)}, u32[]{:S(2)}) copy-start(s32[1024]{0:T(1024)} %param.16) | copy-start | bytes 12292
  13.7 14.8 %copy-start.10 = (s32[1,128]{1,0:T(1,128)S(1)}, s32[1,128]{1,0:T(1,128)}, u32[]{:S(2)}) copy-start(s32[1,128]{1,0:T(1,128)} %param.12) | copy-start | bytes 1540
  24.8 8.9 %copy-start.13 = (s32[128]{0:T(128)S(1)}, s32[128]{0:T(128)}, u32[]{:S(2)}) copy-start(s32[128]{0:T(128)} %param.13) | copy-start | bytes 1540
  28.7 139.0 %copy-start.4 = (bf16[2048,256]{1,0:T(8,128)(2,1)S(1)}, bf16[2048,256]{1,0:T(8,128)(2,1)}, u32[]{:S(2)}) copy-start(bf16[2048,256]{1,0:T(8,128)(2,1)} %all-gather.2.cloned.1.call-done) | copy-start | bytes 3145732
  33.6 281.0 %all-reduce.5.cloned.1.call-start = ((), (), s32[]{:S(2)}) async-start(), calls=%async_computation.2 | async-start | bytes 131072 | tf_op jit(solution)/shard_map/psum | solution.py:74
  198.2 11.1 %copy-start.3 = (bf16[3072,1024]{1,0:T(8,128)(2,1)S(1)}, bf16[3072,1024]{1,0:T(8,128)(2,1)}, u32[]{:S(2)}) copy-start(bf16[3072,1024]{1,0:T(8,128)(2,1)} %gather_fusion) | copy-start | bytes 18874372
  202.3 10.0 %collective-permute-start = (bf16[4,24,1024]{2,1,0:T(8,128)(2,1)S(1)}, bf16[4,24,1024]{2,1,0:T(8,128)(2,1)S(1)}, u32[]{:S(2)}, u32[]{:S(2)}) collective-permute-start(bf16[4,24,1024]{2,1,0:T(8,128)(2,1)S(1)} %bitcast.69), channel_id=1, source_target_pairs={{0,2},{2,4},{4,6},{6,8},{8,10},{10,12},{12,14},{14,16},{16,18},{18... | collective-permute-start | bytes 589832 | tf_op jit(solution)/shard_map/ppermute | solution.py:18
  203.1 26.4 %collective-permute-start.1 = (bf16[4,24,1024]{2,1,0:T(8,128)(2,1)S(1)}, bf16[4,24,1024]{2,1,0:T(8,128)(2,1)S(1)}, u32[]{:S(2)}, u32[]{:S(2)}) collective-permute-start(bf16[4,24,1024]{2,1,0:T(8,128)(2,1)S(1)} %bitcast.68), channel_id=1, source_target_pairs={{2,0},{4,2},{6,4},{8,6},{10,8},{12,10},{14,12},{16,14},{18,16},{20... | collective-permute-start | bytes 589832 | tf_op jit(solution)/shard_map/ppermute | solution.py:19
  210.0 32.4 %copy-start.2 = (bf16[128,24,1024]{2,1,0:T(8,128)(2,1)}, bf16[128,24,1024]{2,1,0:T(8,128)(2,1)S(1)}, u32[]{:S(2)}) copy-start(bf16[128,24,1024]{2,1,0:T(8,128)(2,1)S(1)} %broadcast_select_fusion.1) | copy-start | bytes 18874372
  210.0 6.6 %copy-start.5 = (bf16[128,16,24]{2,1,0:T(8,128)(2,1)S(1)}, bf16[128,16,24]{2,1,0:T(8,128)(2,1)}, u32[]{:S(2)}) copy-start(bf16[128,16,24]{2,1,0:T(8,128)(2,1)} %copy.19) | copy-start | bytes 294916
  216.6 4.3 %copy-start.6 = (bf16[128,16,24]{2,1,0:T(8,128)(2,1)S(1)}, bf16[128,16,24]{2,1,0:T(8,128)(2,1)}, u32[]{:S(2)}) copy-start(bf16[128,16,24]{2,1,0:T(8,128)(2,1)} %copy.21) | copy-start | bytes 294916
  225.2 4.3 %copy-start.7 = (bf16[128,16,24]{2,1,0:T(8,128)(2,1)S(1)}, bf16[128,16,24]{2,1,0:T(8,128)(2,1)}, u32[]{:S(2)}) copy-start(bf16[128,16,24]{2,1,0:T(8,128)(2,1)} %copy.29) | copy-start | bytes 294916
  229.5 4.3 %copy-start.8 = (bf16[128,16,24]{2,1,0:T(8,128)(2,1)S(1)}, bf16[128,16,24]{2,1,0:T(8,128)(2,1)}, u32[]{:S(2)}) copy-start(bf16[128,16,24]{2,1,0:T(8,128)(2,1)} %copy.31) | copy-start | bytes 294916
  233.8 4.3 %copy-start.9 = (bf16[128,16,24]{2,1,0:T(8,128)(2,1)S(1)}, bf16[128,16,24]{2,1,0:T(8,128)(2,1)}, u32[]{:S(2)}) copy-start(bf16[128,16,24]{2,1,0:T(8,128)(2,1)} %copy.33) | copy-start | bytes 294916
  246.7 69.6 %copy-start.1 = (f32[256,256]{1,0:T(8,128)S(1)}, f32[256,256]{1,0:T(8,128)}, u32[]{:S(2)}) copy-start(f32[256,256]{1,0:T(8,128)} %param.11) | copy-start | bytes 786436
Sparse Core Ops, SparseCore 0:
  9.7 15.3 all-gather.1
  33.7 130.9 all-reduce.2
  294.2 20.3 all-reduce.4
where the time goes:
time: 323 us
  waiting for transfers between devices  154 us (48%)
  matrix products  94 us (29%)
  local copies, waits for them, and re-layouts  44.5 us (14%)
  between operations  14.1 us (4%)
  other arithmetic  8.7 us (3%)
  starting transfers between devices  7.08 us (2%)
    psum x1, waiting for transfers between devices, local(): inner_products = lax.psum(inner_products, 'row')  131 us
    dot_general x1, matrix products, local(): jnp.einsum('ain,ajn->aij', weighted, rounded, preferred_element_type=jnp....  46.4 us
    dot_general x8, matrix products, local(): jnp.einsum('aij,ajn->ain', blocks, neighbours, preferred_element_type=jnp...  34.3 us
    psum x1, waiting for transfers between devices, local(): lax.psum(partial_value.astype(jnp.bfloat16), 'col').astype(jnp.float32)  20.5 us
    gather x1, local copies, waits for them, and re-layouts, local(): jnp.take(vectors, row_index.reshape(-1), axis=0, mode='fill', fill_value=0)  18.7 us
    unnamed x40, local copies, waits for them, and re-layouts  14.7 us
    select_n x9, local copies, waits for them, and re-layouts, local(): jnp.where(block_present[:, relative, None, None] > 0, blocks, jnp.zeros_l...  7.69 us
  transfers between devices with their start and end apart: 5, of which 3 were waited for; matrix products, arithmetic and copies ran while one was open for 12% of the time, Pallas kernels for 0%

commit v1 on v0

--- a/solution.py
+++ b/solution.py
@@ -2,6 +2,7 @@
 import jax.numpy as jnp
 from jax import lax
 from jax.sharding import PartitionSpec as P
+from jax.lax import all_gather
 
 NPMAX = 16
 BMAX = 24
@@ -34,7 +35,8 @@
     cols_here = vectors_in.shape[1]
     whole_panel = lax.all_gather(panel, "col", axis=1, tiled=True)
     inner_products = panel_product(whole_panel, vectors_in)
-    inner_products = lax.psum(inner_products, "row")
+    tile_out = all_gather(inner_products, axis_name="row")
+    inner_products = jnp.sum(tile_out, 0)
     mixing = jnp.dot(factor.T, inner_products, precision=lax.Precision.HIGHEST).astype(jnp.bfloat16)
     update = jnp.dot(whole_panel, mixing, preferred_element_type=jnp.float32)
     vectors = (vectors_in.astype(jnp.float32) - update).astype(jnp.bfloat16)

time: 323 us -> 486 us (1.50)
  waiting for transfers between devices: 154 us -> 302 us
  other arithmetic: 8.7 us -> 27.2 us
    all_gather x0 -> x1, waiting for transfers between devices: none -> 261 us  [local(): tile_out = all_gather(inner_products, axis_name='row')]
    psum x1 -> x0, waiting for transfers between devices: 131 us -> none  [local(): inner_products = lax.psum(inner_products, 'row')]
    reduce_sum x0 -> x1, other arithmetic: none -> 20.8 us  [local(): inner_products = jnp.sum(tile_out, 0)]
    all_gather x1, waiting for transfers between devices: 0.02 us -> 17.1 us  [local(): whole_panel = lax.all_gather(panel, 'col', axis=1, tiled=True)]
    unnamed x40 -> x42, local copies, waits for them, and re-layouts: 14.7 us -> 14.8 us
  transfers between devices with their start and end apart: 5 -> 5, of which waited for: 3 -> 4; matrix products, arithmetic and copies ran while one was open for 12% -> 7% of each run, Pallas kernels for 0% -> 0%
where the time goes in v1:
time: 486 us
  waiting for transfers between devices  302 us (62%)
  matrix products  93 us (19%)
  local copies, waits for them, and re-layouts  42.6 us (9%)
  other arithmetic  27.2 us (6%)
  between operations  14.1 us (3%)
  starting transfers between devices  7.08 us (1%)
    all_gather x1, waiting for transfers between devices, local(): tile_out = all_gather(inner_products, axis_name='row')  261 us
    dot_general x1, matrix products, local(): jnp.einsum('ain,ajn->aij', weighted, rounded, preferred_element_type=jnp....  46.4 us
    dot_general x8, matrix products, local(): jnp.einsum('aij,ajn->ain', blocks, neighbours, preferred_element_type=jnp...  34.3 us
    reduce_sum x1, other arithmetic, local(): inner_products = jnp.sum(tile_out, 0)  20.8 us
    psum x1, waiting for transfers between devices, local(): lax.psum(partial_value.astype(jnp.bfloat16), 'col').astype(jnp.float32)  19.5 us
    gather x1, local copies, waits for them, and re-layouts, local(): jnp.take(vectors, row_index.reshape(-1), axis=0, mode='fill', fill_value=0)  18.6 us
    all_gather x1, waiting for transfers between devices, local(): whole_panel = lax.all_gather(panel, 'col', axis=1, tiled=True)  17.1 us
    unnamed x42, local copies, waits for them, and re-layouts  14.8 us
  transfers between devices with their start and end apart: 5, of which 4 were waited for; matrix products, arithmetic and copies ran while one was open for 7% of the time, Pallas kernels for 0%

profile of v1, /device:TPU:1, one launch (start us, length us, event | category | flops | bytes accessed | tf_op | source)
XLA Modules:
  0.0 485.7 jit_solution(17822947373728774942)
XLA Ops:
  7.2 0.0 copy-start
  7.2 0.0 all-gather.4.cloned.1.call-start
  7.2 0.7 all-gather.4.cloned.1.call-update
  7.9 0.0 all-gather.6.cloned.1.call-start
  8.0 17.1 %all-gather.4.cloned.1.call-done = bf16[2048,256]{1,0:T(8,128)(2,1)} async-done(((bf16[2048,128]{1,0:T(8,128)(2,1)}), bf16[2048,256]{1,0:T(8,128)(2,1)}) %all-gather.4.cloned.1.call-update) | async-done | bytes 1048592 | tf_op jit(solution)/shard_map/all_gather | solution.py:36
  25.0 4.8 fusion.51
  29.8 0.0 all-gather.6.cloned.1.call-update
  29.8 0.0 all-reduce.2.cloned.1.call-start
  29.9 6.5 %copy.15 = bf16[2048,1024]{0,1:T(8,128)(2,1)} copy(bf16[2048,1024]{1,0:T(8,128)(2,1)} %param.9) | data formatting | bytes 8388608 | tf_op args[0]
  36.4 0.0 copy-done.10
  36.4 0.1 copy.17
  36.5 0.2 reduce-window.8
  36.7 0.1 reduce
  36.8 0.1 add_select_fusion
  36.9 0.1 select_n.82
  37.0 0.1 select_n.80
  37.1 0.1 fusion.48
  37.2 0.1 copy.41
  37.4 0.1 copy.42
  37.6 0.4 copy.23
  38.0 0.1 copy.40
  38.1 0.1 copy.39
  38.3 1.2 copy.19
  39.5 1.2 copy.21
  40.8 0.4 copy.25
  41.2 0.1 copy.44
  41.3 0.1 copy.45
  41.5 1.2 copy.29
  42.7 1.2 copy.31
  43.9 0.1 copy.46
  44.0 0.1 copy.47
  44.1 1.2 copy.33
  45.3 0.4 copy.35
  45.8 0.1 copy.43
  45.9 0.4 copy.27
  46.4 0.1 compare_and_fusion
  46.6 0.1 fusion.38
  46.6 260.9 %all-gather.6.cloned.1.call-done = f32[16384,1024]{1,0:T(8,128)} async-done(((f32[256,1024]{1,0:T(8,128)}), f32[16384,1024]{1,0:T(8,128)}) %all-gather.6.cloned.1.call-update) | async-done | bytes 67108880 | tf_op jit(solution)/shard_map/all_gather | solution.py:38
  307.5 20.8 %reduce_sum.9 = f32[256,1024]{1,0:T(8,128)S(1)} reduce(f32[64,256,1024]{2,1,0:T(8,128)} %bitcast, f32[]{:T(128)} %constant.10.clone.1), dimensions={0}, to_apply=%region_0.0 | reduce | flops 16515072 | bytes 68157440 | tf_op jit(solution)/shard_map/reduce_sum | solution.py:39
  328.3 1.8 convolution_convert_fusion
  330.1 5.8 %fusion = bf16[2048,1024]{0,1:T(8,128)(2,1)} fusion(bf16[2048,1024]{0,1:T(8,128)(2,1)} %copy.15, bf16[1024,256]{1,0:T(8,128)(2,1)S(1)} %convolution_convert_fusion, bf16[2048,256]{1,0:T(8,128)(2,1)} %all-gather.4.cloned.1.call-done), kind=kOutput, calls=%fused_computation.8 | convolution fusion | flops 1080033280 | bytes 9961472 | tf_op jit(solution)/shard_map/dot_general | solution.py:41
  335.9 6.4 %copy.37 = bf16[2048,1024]{1,0:T(8,128)(2,1)} copy(bf16[2048,1024]{0,1:T(8,128)(2,1)} %fusion) | data formatting | bytes 8388608
  342.3 18.6 %gather_fusion = bf16[3072,1024]{1,0:T(8,128)(2,1)} fusion(bf16[2048,1024]{1,0:T(8,128)(2,1)} %copy.37, s32[3072]{0:T(1024)S(1)} %broadcast_clamp_fusion), kind=kCustom, calls=%fused_computation | custom fusion | bytes 12595200 | tf_op jit(solution)/shard_map/jit(_take)/gather | solution.py:50
  360.8 4.1 broadcast_select_fusion
  364.9 1.3 collective-permute-start
  366.2 5.7 %collective-permute-start.1 = (bf16[4,24,1024]{2,1,0:T(8,128)(2,1)S(1)}, bf16[4,24,1024]{2,1,0:T(8,128)(2,1)S(1)}, u32[]{:S(2)}, u32[]{:S(2)}) collective-permute-start(bf16[4,24,1024]{2,1,0:T(8,128)(2,1)S(1)} %bitcast.69), channel_id=1, source_target_pairs={{2,0},{4,2},{6,4},{8,6},{10,8},{12,10},{14,12},{16,14},{18,16},{20... | collective-permute-start | bytes 589832 | tf_op jit(solution)/shard_map/ppermute | solution.py:20
  371.9 0.7 broadcast_select_fusion.1
  372.6 3.6 collective-permute-done
  376.2 4.3 fusion.12
  380.5 4.2 fusion.15
  384.8 4.3 fusion.18
  389.1 4.3 fusion.25
  393.4 0.0 collective-permute-done.1
  393.4 4.3 fusion.6
  397.7 4.3 fusion.9
  402.0 4.3 fusion.3
  406.3 0.0 copy-done.2
  406.3 4.3 fusion.20
  410.5 46.4 %fusion.37 = bf16[128,16,16]{2,1,0:T(8,128)(2,1)S(1)} fusion(f32[128,16,1024]{2,1,0:T(8,128)} %fusion.20, f32[128,16,1024]{2,1,0:T(8,128)} %fusion.3, f32[128,16,1024]{2,1,0:T(8,128)} %fusion.9, f32[128,16,1024]{2,1,0:T(8,128)} %fusion.6, f32[128,16,1024]{2,1,0:T(8,128)} %fusion.25, f32[128,16,1024]{2,1,0:T(8,128)} %fusion.12, ...), kind=kOutput, calls=%fused_computation.46 | convolution fusion | flops 316702720 | bytes 73576448 | tf_op jit(solution)/shard_map/ain,ajn->aij/dot_general | solution.py:72
  456.9 1.1 copy.36
  458.0 0.0 all-reduce.2.cloned.1.call-update
  458.0 19.5 %all-reduce.2.cloned.1.call-done = bf16[128,256]{0,1:T(8,128)(2,1)} async-done(((bf16[128,256]{0,1:T(8,128)(2,1)}), bf16[128,256]{0,1:T(8,128)(2,1)}) %all-reduce.2.cloned.1.call-update) | async-done | bytes 65552 | tf_op jit(solution)/shard_map/psum | solution.py:76
  477.5 0.9 dynamic-slice_convert_fusion
  478.4 0.7 copy.38
  (39 shorter events, 0.2 us)
Async XLA Ops:
  7.2 321.1 %copy-start = (f32[256,256]{1,0:T(8,128)S(1)}, f32[256,256]{1,0:T(8,128)}, u32[]{:S(2)}) copy-start(f32[256,256]{1,0:T(8,128)} %param.11) | copy-start | bytes 786436
  7.2 17.9 %all-gather.4.cloned.1.call-start = ((), (), s32[]{:S(2)}) async-start(), calls=%async_computation | async-start | bytes 1572864 | tf_op jit(solution)/shard_map/all_gather | solution.py:36
  7.9 299.6 %all-gather.6.cloned.1.call-start = ((), (), s32[]{:S(2)}) async-start(), calls=%async_computation.2 | async-start | bytes 68157440 | tf_op jit(solution)/shard_map/all_gather | solution.py:38
  29.8 6.6 %copy-start.10 = (s32[1,128]{1,0:T(1,128)S(1)}, s32[1,128]{1,0:T(1,128)}, u32[]{:S(2)}) copy-start(s32[1,128]{1,0:T(1,128)} %param.12) | copy-start | bytes 1540
  29.8 7.3 %copy-start.4 = (bf16[128,9,384]{2,0,1:T(8,128)(2,1)S(1)}, bf16[128,9,384]{2,0,1:T(8,128)(2,1)}, u32[]{:S(2)}) copy-start(bf16[128,9,384]{2,0,1:T(8,128)(2,1)} %param.14) | copy-start | bytes 2654212
  29.8 7.7 %copy-start.13 = (s32[128,9]{0,1:T(8,128)S(1)}, s32[128,9]{0,1:T(8,128)}, u32[]{:S(2)}) copy-start(s32[128,9]{0,1:T(8,128)} %param.15) | copy-start | bytes 13828
  29.8 447.7 %all-reduce.2.cloned.1.call-start = ((), (), s32[]{:S(2)}) async-start(), calls=%async_computation.1 | async-start | bytes 131072 | tf_op jit(solution)/shard_map/psum | solution.py:76
  36.4 9.9 %copy-start.11 = (f32[1024]{0:T(1024)S(1)}, f32[1024]{0:T(1024)}, u32[]{:S(2)}) copy-start(f32[1024]{0:T(1024)} %param.17) | copy-start | bytes 12292
  36.4 10.0 %copy-start.12 = (s32[1024]{0:T(1024)S(1)}, s32[1024]{0:T(1024)}, u32[]{:S(2)}) copy-start(s32[1024]{0:T(1024)} %param.16) | copy-start | bytes 12292
  36.4 10.1 %copy-start.14 = (s32[128]{0:T(128)S(1)}, s32[128]{0:T(128)}, u32[]{:S(2)}) copy-start(s32[128]{0:T(128)} %param.13) | copy-start | bytes 1540
  360.8 11.1 %copy-start.3 = (bf16[3072,1024]{1,0:T(8,128)(2,1)S(1)}, bf16[3072,1024]{1,0:T(8,128)(2,1)}, u32[]{:S(2)}) copy-start(bf16[3072,1024]{1,0:T(8,128)(2,1)} %gather_fusion) | copy-start | bytes 18874372
  364.9 11.3 %collective-permute-start = (bf16[4,24,1024]{2,1,0:T(8,128)(2,1)S(1)}, bf16[4,24,1024]{2,1,0:T(8,128)(2,1)S(1)}, u32[]{:S(2)}, u32[]{:S(2)}) collective-permute-start(bf16[4,24,1024]{2,1,0:T(8,128)(2,1)S(1)} %bitcast.70), channel_id=1, source_target_pairs={{0,2},{2,4},{4,6},{6,8},{8,10},{10,12},{12,14},{14,16},{16,18},{18... | collective-permute-start | bytes 589832 | tf_op jit(solution)/shard_map/ppermute | solution.py:19
  366.2 27.2 %collective-permute-start.1 = (bf16[4,24,1024]{2,1,0:T(8,128)(2,1)S(1)}, bf16[4,24,1024]{2,1,0:T(8,128)(2,1)S(1)}, u32[]{:S(2)}, u32[]{:S(2)}) collective-permute-start(bf16[4,24,1024]{2,1,0:T(8,128)(2,1)S(1)} %bitcast.69), channel_id=1, source_target_pairs={{2,0},{4,2},{6,4},{8,6},{10,8},{12,10},{14,12},{16,14},{18,16},{20... | collective-permute-start | bytes 589832 | tf_op jit(solution)/shard_map/ppermute | solution.py:20
  372.6 33.7 %copy-start.2 = (bf16[128,24,1024]{2,1,0:T(8,128)(2,1)}, bf16[128,24,1024]{2,1,0:T(8,128)(2,1)S(1)}, u32[]{:S(2)}) copy-start(bf16[128,24,1024]{2,1,0:T(8,128)(2,1)S(1)} %broadcast_select_fusion.1) | copy-start | bytes 18874372
  372.6 7.9 %copy-start.5 = (bf16[128,16,24]{2,1,0:T(8,128)(2,1)S(1)}, bf16[128,16,24]{2,1,0:T(8,128)(2,1)}, u32[]{:S(2)}) copy-start(bf16[128,16,24]{2,1,0:T(8,128)(2,1)} %copy.19) | copy-start | bytes 294916
  380.5 4.2 copy-start.6
  389.1 4.3 copy-start.7
  393.4 4.3 copy-start.8
  397.7 4.3 copy-start.9
  410.5 68.6 %copy-start.1 = (f32[256,256]{1,0:T(8,128)S(1)}, f32[256,256]{1,0:T(8,128)}, u32[]{:S(2)}) copy-start(f32[256,256]{1,0:T(8,128)} %param.11) | copy-start | bytes 786436
Sparse Core Ops, SparseCore 0:
  9.7 15.3 all-gather.3
  30.0 277.5 all-gather.5
  458.1 19.3 all-reduce.1
